TPU v7x, 256 devices: a whole 4x4x8 slice. The times are simulated.
256 devices in a mesh: dp: 16 (over y, x), seq: 16 (over z, core).
Axes of the slice: x: 4, y: 4, z: 8, core: 2. Of those that a mesh axis runs over, the one named last changes fastest.
Arguments:
- ssm_input: bfloat16 [16, 2048, 2048], P('dp', 'seq'), may hold values from -6 to 6
- gate_input: bfloat16 [16, 2048, 2048], P('dp', 'seq'), may hold values from -6 to 6
- grad_gated: bfloat16 [16, 2048, 2048], P('dp', 'seq'), may hold values from -6 to 6
- x_proj: bfloat16 [2048, 96], replicated, may hold values from -0.125 to 0.125
- dt_proj: bfloat16 [64, 2048], replicated, may hold values from -0.75 to 0.75
- dt_bias: float32 [2048], replicated, may hold values from -14 to -2
- fid_bias: float32 [2, 2048], replicated, may hold values from -3 to 3
- a_log: float32 [2048, 16], replicated, may hold values from 0 to 2.77
- skip_gain: float32 [2048], replicated, may hold values from 0.5 to 1.5
- rec_lengths: int32 [16], P('dp'), may hold values from 512 to 2048, as said below
- fid_labels: int32 [16], P('dp'), may hold values from 0 to 1
Outputs:
- gated: bfloat16 [16, 2048, 2048], P('dp', 'seq')
- grad_input: bfloat16 [16, 2048, 2048], P('dp', 'seq')
- grad_gate: bfloat16 [16, 2048, 2048], P('dp', 'seq')
- grad_x_proj: float32 [2048, 96], P('dp')
- grad_dt_proj: float32 [64, 2048], P(None, 'dp')
- grad_a_log: float32 [2048, 16], P('dp')
- grad_skip: float32 [2048], P('dp')
- grad_dt_bias: float32 [2048], P('dp')
- grad_fid_bias: float32 [2, 2048], P(None, 'dp')
Inputs may be any that keep to these rules, and one draw needn't show every extreme that they name: `rec_lengths`: each record's count of valid time steps; in every draw some record is 2048 long.
All inputs are finite; a program needn't handle non-finite values.
Results may differ from a plain program's by a relative error of at most 0.0068.
Values sent between devices are 32-bit elements; how exact they have to be, the bound alone decides.
A program may use at most 64 MiB of HBM per device.

v0:
```python
import jax
import jax.numpy as jnp
from jax import lax
from jax.sharding import PartitionSpec as P


def passed_along(block, axis, distance):
    devices = range(lax.axis_size(axis))
    route = [(i - distance, i) for i in devices if i - distance in devices]
    return lax.ppermute(block, axis, route)


def run_block(h_now, a_trans, pieces):
    step_blk, b_blk, c_blk, val_blk = pieces
    outputs = []
    for position in range(step_blk.shape[0]):
        decay = jnp.exp(a_trans * step_blk[position][None, :])
        h_now = (
            decay * h_now
            + b_blk[position][:, None] * (step_blk[position] * val_blk[position])[None, :]
        )
        outputs.append(jnp.sum(c_blk[position][:, None] * h_now, axis=0))
    return (h_now, jnp.stack(outputs))


def to_blocks(array, turns):
    return array.reshape((turns, array.shape[0] // turns) + array.shape[1:])


def forward_record(h_start, a_trans, pieces, turns):
    blocks = tuple((to_blocks(piece, turns) for piece in pieces))

    def advance(h_now, blk_pieces):
        h_next, outputs = run_block(h_now, a_trans, blk_pieces)
        return (h_next, (h_now, outputs))

    h_last, (checks, outputs) = lax.scan(advance, h_start, blocks)
    return (h_last, checks, outputs.reshape((-1, outputs.shape[-1])))


def pull_record(stepsize, c_proj, y_grad, a_trans, turns):
    blocks = (to_blocks(stepsize, turns), to_blocks(c_proj, turns), to_blocks(y_grad, turns))

    def pull_retreat(adjoint, blk_pieces):
        step_blk, c_blk, grad_blk = blk_pieces
        for position in range(step_blk.shape[0] - 1, -1, -1):
            gathered = c_blk[position][:, None] * grad_blk[position][None, :] + adjoint
            adjoint = jnp.exp(a_trans * step_blk[position][None, :]) * gathered
        return (adjoint, None)

    adjoint, _ = lax.scan(pull_retreat, jnp.zeros_like(a_trans), blocks, reverse=True)
    return adjoint


def backward_record(checks, end_grad, a_trans, pieces, y_grad, turns):
    blocks = tuple((to_blocks(piece, turns) for piece in pieces))
    grad_blocks = to_blocks(y_grad, turns)

    def backward_retreat(carry, inputs):
        adjoint, a_total = carry
        h_in, blk_pieces, grad_blk = inputs
        _, block_back = jax.vjp(run_block, h_in, a_trans, blk_pieces)
        h_grad, a_part, piece_grads = block_back((adjoint, grad_blk))
        return ((h_grad, a_total + a_part), piece_grads)

    (_, a_grad), piece_grads = lax.scan(
        backward_retreat,
        (end_grad, jnp.zeros_like(a_trans)),
        (checks, blocks, grad_blocks),
        reverse=True,
    )
    flat = tuple((grad.reshape((-1,) + grad.shape[2:]) for grad in piece_grads))
    return flat + (a_grad,)


def per_device(
    ssm_input,
    gate_input,
    grad_gated,
    x_proj,
    dt_proj,
    dt_bias,
    fid_bias,
    a_log,
    skip_gain,
    rec_lengths,
    fid_labels,
):
    records, seg_len, channels = ssm_input.shape
    low_rank = dt_proj.shape[0]
    states = a_log.shape[1]
    fidelities = fid_bias.shape[0]
    turns = min(16, seg_len)
    projected = jnp.einsum("rle,ek->rlk", ssm_input, x_proj, preferred_element_type=jnp.float32)
    low = projected[:, :, :low_rank].astype(jnp.bfloat16)
    b_proj = projected[:, :, low_rank : low_rank + states]
    c_proj = projected[:, :, low_rank + states :]
    onehot = (fid_labels[:, None] == jnp.arange(fidelities, dtype=jnp.int32)[None, :]).astype(
        jnp.float32
    )
    fid_shift = jnp.dot(onehot, fid_bias, precision=lax.Precision.HIGHEST)
    dt_raw = (
        jnp.einsum("rlk,ke->rle", low, dt_proj, preferred_element_type=jnp.float32)
        + dt_bias
        + fid_shift[:, None, :]
    )
    positions = lax.axis_index("seq") * seg_len + jnp.arange(seg_len, dtype=jnp.int32)
    live = (positions[None, :] < rec_lengths[:, None]).astype(jnp.float32)[:, :, None]
    stepsize = jax.nn.softplus(dt_raw) * live
    a_matrix = -jnp.exp(a_log)
    a_trans = a_matrix.T
    values = ssm_input.astype(jnp.float32)
    s_total = jnp.sum(stepsize, axis=1)

    def zero_ends(pieces):
        h_last, _, _ = forward_record(jnp.zeros_like(a_trans), a_trans, pieces, turns)
        return h_last

    h_end = lax.map(zero_ends, (stepsize, b_proj, c_proj, values))
    gate_value = gate_input.astype(jnp.float32)
    gate_sigmoid = jax.nn.sigmoid(gate_value)
    gate_silu = gate_value * gate_sigmoid
    out_grad = grad_gated.astype(jnp.float32) * live
    y_grad = out_grad * gate_silu

    def pulls(pieces):
        step_rec, c_rec, grad_rec = pieces
        return pull_record(step_rec, c_rec, grad_rec, a_trans, turns)

    h_pull = lax.map(pulls, (stepsize, c_proj, y_grad))
    decay_total = jnp.exp(a_trans[None] * s_total[:, None, :])

    def forward_turn(turn, incoming):
        return passed_along(decay_total * incoming + h_end, "seq", 1)

    def backward_turn(turn, incoming):
        return passed_along(h_pull + decay_total * incoming, "seq", -1)

    h_start = lax.fori_loop(0, lax.axis_size("seq") - 1, forward_turn, jnp.zeros_like(h_end))
    end_grad = lax.fori_loop(0, lax.axis_size("seq") - 1, backward_turn, jnp.zeros_like(h_pull))

    def full_forward(pieces):
        start_rec, step_rec, b_rec, c_rec, val_rec = pieces
        _, checks, outputs = forward_record(
            start_rec, a_trans, (step_rec, b_rec, c_rec, val_rec), turns
        )
        return (checks, outputs)

    checks, y_ssm = lax.map(full_forward, (h_start, stepsize, b_proj, c_proj, values))
    y_full = y_ssm + skip_gain * values
    gated = (y_full * gate_silu * live).astype(jnp.bfloat16)
    grad_gate = (
        out_grad * y_full * (gate_sigmoid * (1.0 + gate_value * (1.0 - gate_sigmoid)))
    ).astype(jnp.bfloat16)

    def full_backward(pieces):
        check_rec, end_rec, step_rec, b_rec, c_rec, val_rec, grad_rec = pieces
        return backward_record(
            check_rec, end_rec, a_trans, (step_rec, b_rec, c_rec, val_rec), grad_rec, turns
        )

    step_grad, b_grad, c_grad, u_grad, a_grads = lax.map(
        full_backward, (checks, end_grad, stepsize, b_proj, c_proj, values, y_grad)
    )
    a_grad = jnp.sum(a_grads, axis=0).T
    dt_grad = step_grad * live * jax.nn.sigmoid(dt_raw)
    dt_grad_b = dt_grad.astype(jnp.bfloat16)
    dt_proj_part = jnp.einsum("rlk,rle->ek", low, dt_grad_b, preferred_element_type=jnp.float32)
    low_grad = jnp.einsum("rle,ke->rlk", dt_grad_b, dt_proj, preferred_element_type=jnp.float32)
    proj_grad = jnp.concatenate([low_grad, b_grad, c_grad], axis=2).astype(jnp.bfloat16)
    x_proj_part = jnp.einsum(
        "rle,rlk->ek", ssm_input, proj_grad, preferred_element_type=jnp.float32
    )
    input_grad = (
        u_grad
        + y_grad * skip_gain
        + jnp.einsum("rlk,ek->rle", proj_grad, x_proj, preferred_element_type=jnp.float32)
    )
    grad_input = input_grad.astype(jnp.bfloat16)
    dt_sums = jnp.sum(dt_grad, axis=1)
    packed = jnp.concatenate(
        [
            x_proj_part,
            dt_proj_part,
            a_grad * a_matrix,
            jnp.sum(y_grad * values, axis=(0, 1))[:, None],
            jnp.sum(dt_sums, axis=0)[:, None],
            jnp.dot(dt_sums.T, onehot, precision=lax.Precision.HIGHEST),
        ],
        axis=1,
    )
    totals = lax.psum(packed, "seq")
    shares = lax.psum_scatter(totals, "dp", scatter_dimension=0, tiled=True)
    col_x = low_rank + 2 * states
    col_dt = col_x + low_rank
    col_a = col_dt + states
    grad_x_proj = shares[:, :col_x]
    grad_dt_proj = shares[:, col_x:col_dt].T
    grad_a_log = shares[:, col_dt:col_a]
    grad_skip = shares[:, col_a]
    grad_dt_bias = shares[:, col_a + 1]
    grad_fid_bias = shares[:, col_a + 2 :].T
    return (
        gated,
        grad_input,
        grad_gate,
        grad_x_proj,
        grad_dt_proj,
        grad_a_log,
        grad_skip,
        grad_dt_bias,
        grad_fid_bias,
    )


def solution(mesh):
    in_specs = (
        P("dp", "seq", None),
        P("dp", "seq", None),
        P("dp", "seq", None),
        P(),
        P(),
        P(),
        P(),
        P(),
        P(),
        P("dp"),
        P("dp"),
    )
    out_specs = (
        P("dp", "seq", None),
        P("dp", "seq", None),
        P("dp", "seq", None),
        P("dp", None),
        P(None, "dp"),
        P("dp", None),
        P("dp"),
        P("dp"),
        P(None, "dp"),
    )
    return jax.shard_map(
        per_device, mesh=mesh, in_specs=in_specs, out_specs=out_specs, check_vma=False
    )
```

profile of v0, /device:TPU:1, one launch (start us, length us, event | category | flops | bytes accessed | tf_op | source)
XLA Modules:
  0.0 812.1 jit_solution(1618265109441323945)
XLA Ops:
  14.2 38.7 %while.126 = (s32[]{:T(128)}, f32[16,2048]{1,0:T(8,128)S(1)}, f32[16,8,2048]{2,1,0:T(8,128)}, f32[16,2048]{1,0:T(8,128)S(1)}, f32[16,8,16]{2,1,0:T(8,128)}, /*in...) while((s32[]{:T(128)}, f32[16,2048]{1,0:T(8,128)S(1)}, ...), condition=%wide.region_2.3_spmd.clone, body=%wide.region_1.2_spmd.clone.sunk | while | flops 1097738 | bytes 985871 | solution.py:37
  54.0 95.3 %while.123 = (s32[]{:T(128)}, f32[1,16,2048]{2,1,0:T(8,128)S(1)}, f32[1,16,2048]{2,1,0:T(8,128)S(1)}, f32[1,16,2048]{2,1,0:T(8,128)S(1)}, s32[]{:T(128)}) while((s32[]{:T(128)}, f32[1,16,2048]{2,1,0:T(8,128)S(1)}, f32[1,16,2048]{2,1,0:T(8,128)S(1)}, f32[1,16,2048]{2,1,0:T(8,128)S(1)}, s32[]{:T(128)}) %tuple.429), condition=%wide.region_4.5_spmd, body=%wide.region_3.4_spmd.sunk | while | flops 65538 | bytes 1048677 | solution.py:139
  54.0 4.9 collective-permute-start
  150.3 73.6 %while.124 = (s32[]{:T(128)}, f32[16,2048]{1,0:T(8,128)S(1)}, f32[16,16,2048]{2,1,0:T(8,128)}, f32[16,8,2048]{2,1,0:T(8,128)}, f32[16,8,2048]{2,1,0:T(8,128)}, /...) while((s32[]{:T(128)}, f32[16,2048]{1,0:T(8,128)S(1)}, ...), condition=%wide.region_14.15_spmd, body=%wide.region_5.0_spmd.sunk | while | flops 2359305 | bytes 2333341 | solution.py:37
  228.0 70.4 %while.127 = (s32[]{:T(128)}, f32[16,2048]{1,0:T(8,128)S(1)}, f32[16,8,2048]{2,1,0:T(8,128)}, f32[16,2048]{1,0:T(8,128)S(1)}, f32[16,8,16]{2,1,0:T(8,128)}, /*in...) while((s32[]{:T(128)}, f32[16,2048]{1,0:T(8,128)S(1)}, ...), condition=%wide.region_16.17_spmd.clone, body=%wide.region_15.16_spmd.clone.sunk | while | flops 1081355 | bytes 789283 | solution.py:51
  299.4 114.7 %while.125 = (s32[]{:T(128)}, f32[1,16,2048]{2,1,0:T(8,128)S(1)}, f32[1,16,2048]{2,1,0:T(8,128)S(1)}, f32[1,16,2048]{2,1,0:T(8,128)S(1)}, s32[]{:T(128)}) while((s32[]{:T(128)}, f32[1,16,2048]{2,1,0:T(8,128)S(1)}, f32[1,16,2048]{2,1,0:T(8,128)S(1)}, f32[1,16,2048]{2,1,0:T(8,128)S(1)}, s32[]{:T(128)}) %tuple.428), condition=%wide.region_18.19_spmd, body=%wide.region_17.18_spmd.sunk | while | flops 65538 | bytes 1048677 | solution.py:140
  301.4 5.7 collective-permute-done.1
  309.1 5.4 collective-permute-done.1
  316.5 6.3 collective-permute-done.1
  324.7 5.4 collective-permute-done.1
  332.1 6.3 collective-permute-done.1
  340.3 5.4 collective-permute-done.1
  347.7 6.3 collective-permute-done.1
  355.9 5.6 collective-permute-done.1
  363.5 5.6 collective-permute-done.1
  371.0 5.6 collective-permute-done.1
  378.5 5.6 collective-permute-done.1
  386.0 5.6 collective-permute-done.1
  393.6 5.6 collective-permute-done.1
  401.1 5.6 collective-permute-done.1
  408.6 5.6 collective-permute-done.1
  416.4 175.0 %while.128 = (s32[]{:T(128)}, f32[16,2048]{1,0:T(8,128)S(1)}, f32[16,2048]{1,0:T(8,128)S(1)}, f32[16,8,2048]{2,1,0:T(8,128)}, bf16[16,8,16]{2,1,0:T(8,128)(2,1)S...) while((s32[]{:T(128)}, f32[16,2048]{1,0:T(8,128)S(1)}, ...), condition=%wide.region_52.53_spmd.clone, body=%wide.region_19.52_spmd.clone.sunk | while | flops 8701451 | bytes 6086559 | solution.py:66
  598.1 93.7 %reduce-scatter.2.cloned.1.call-done = f32[128,180]{0,1:T(8,128)} async-done(((f32[2048,180]{0,1:T(8,128)}), f32[128,180]{0,1:T(8,128)}) %reduce-scatter.2.cloned.1.call-update) | async-done | bytes 92176 | tf_op jit(solution)/shard_map/reduce_scatter | solution.py:193
  694.3 104.4 %all-reduce.42.cloned.1.call-done = f32[128,180]{0,1:T(8,128)} async-done(((f32[128,180]{0,1:T(8,128)}), f32[128,180]{0,1:T(8,128)}) %all-reduce.42.cloned.1.call-update) | async-done | bytes 92176 | tf_op jit(solution)/shard_map/psum | solution.py:192
  (1217 shorter events, 501.9 us)
Async XLA Ops:
  7.2 684.6 %reduce-scatter.2.cloned.1.call-start = ((), (), s32[]{:S(2)}) async-start(), calls=%async_computation.1 | async-start | bytes 1601536 | tf_op jit(solution)/shard_map/reduce_scatter | solution.py:193
  54.0 6.9 collective-permute-start
  60.9 6.3 collective-permute-start
  73.5 6.3 collective-permute-start
  92.5 6.3 collective-permute-start
  105.1 6.3 collective-permute-start
  124.0 6.3 collective-permute-start
  136.7 6.3 collective-permute-start
  299.5 7.6 collective-permute-start.1
  307.1 7.4 collective-permute-start.1
  314.5 8.2 %collective-permute-start.1 = (f32[1,16,2048]{2,1,0:T(8,128)S(1)}, f32[1,16,2048]{2,1,0:T(8,128)S(1)}, u32[]{:S(2)}, u32[]{:S(2)}) collective-permute-start(f32[1,16,2048]{2,1,0:T(8,128)S(1)} %multiply_add_fusion.34), channel_id=1, source_target_pairs={{1,0},{2,1},{3,2},{4,3},{5,4},{6,5},{7,6},{8,7},{9,8},{10,9},{11,1... | collective-permute-start | bytes 393224 | tf_op jit(solution)/shard_map/while/body/eval_jaxpr/ppermute | solution.py:10
  322.8 7.4 collective-permute-start.1
  330.1 8.2 %collective-permute-start.1 = (f32[1,16,2048]{2,1,0:T(8,128)S(1)}, f32[1,16,2048]{2,1,0:T(8,128)S(1)}, u32[]{:S(2)}, u32[]{:S(2)}) collective-permute-start(f32[1,16,2048]{2,1,0:T(8,128)S(1)} %multiply_add_fusion.34), channel_id=1, source_target_pairs={{1,0},{2,1},{3,2},{4,3},{5,4},{6,5},{7,6},{8,7},{9,8},{10,9},{11,1... | collective-permute-start | bytes 393224 | tf_op jit(solution)/shard_map/while/body/eval_jaxpr/ppermute | solution.py:10
  338.4 7.4 collective-permute-start.1
  345.8 8.2 %collective-permute-start.1 = (f32[1,16,2048]{2,1,0:T(8,128)S(1)}, f32[1,16,2048]{2,1,0:T(8,128)S(1)}, u32[]{:S(2)}, u32[]{:S(2)}) collective-permute-start(f32[1,16,2048]{2,1,0:T(8,128)S(1)} %multiply_add_fusion.34), channel_id=1, source_target_pairs={{1,0},{2,1},{3,2},{4,3},{5,4},{6,5},{7,6},{8,7},{9,8},{10,9},{11,1... | collective-permute-start | bytes 393224 | tf_op jit(solution)/shard_map/while/body/eval_jaxpr/ppermute | solution.py:10
  354.0 7.5 collective-permute-start.1
  361.5 7.5 collective-permute-start.1
  369.1 7.5 collective-permute-start.1
  376.6 7.5 collective-permute-start.1
  384.1 7.5 collective-permute-start.1
  391.6 7.5 collective-permute-start.1
  399.1 7.5 collective-permute-start.1
  406.7 7.5 collective-permute-start.1
  598.0 200.6 %all-reduce.42.cloned.1.call-start = ((), (), s32[]{:S(2)}) async-start(), calls=%async_computation.2 | async-start | bytes 188416 | tf_op jit(solution)/shard_map/psum | solution.py:192
  (30 other events, 1107.3 us)
Sparse Core Ops, SparseCore 0:
  598.2 93.5 reduce-scatter.1
  694.1 104.5 all-reduce.41
where the time goes:
time: 823 us; the launch traced here: 812 us
  waiting for transfers between devices  312 us (38%)
  local copies, waits for them, and re-layouts  223 us (27%)
  other arithmetic  155 us (19%)
  starting transfers between devices  94.8 us (12%)
  between operations  15.8 us (2%)
    ppermute x30, waiting for transfers between devices, passed_along(): return lax.ppermute(block, axis, route)  114 us
    psum x1, waiting for transfers between devices, per_device(): totals = lax.psum(packed, 'seq')  104 us
    ppermute x30, starting transfers between devices, passed_along(): return lax.ppermute(block, axis, route)  94.7 us
    reduce_scatter x1, waiting for transfers between devices, per_device(): shares = lax.psum_scatter(totals, 'dp', scatter_dimension=0, tiled=True)  93.7 us
    slice x48, local copies, waits for them, and re-layouts, run_block(): val_blk[position]  69.5 us
    dynamic_slice x64, local copies, waits for them, and re-layouts, forward_record(): h_last, (checks, outputs) = lax.scan(advance, h_start, blocks)  44.5 us
    reduce_sum x80, other arithmetic, run_block(): outputs.append(jnp.sum(c_blk[position][:, None] * h_now, axis=0))  36.7 us
    reduce_sum x32, other arithmetic, run_block(): decay = jnp.exp(a_trans * step_blk[position][None, :])  33.4 us
  transfers between devices with their start and end apart: 32, of which 32 were waited for; matrix products, arithmetic and copies ran while one was open for 0% of the time, Pallas kernels for 0%

commit v1 on v0

--- a/solution.py
+++ b/solution.py
@@ -189,7 +189,9 @@
         ],
         axis=1,
     )
-    totals = lax.psum(packed, "seq")
+    totals = packed
+    for hop in (1, 2, 4, 8):
+        totals = totals + lax.ppermute(totals, "seq", [(dev, dev ^ hop) for dev in range(16)])
     shares = lax.psum_scatter(totals, "dp", scatter_dimension=0, tiled=True)
     col_x = low_rank + 2 * states
     col_dt = col_x + low_rank

time: 823 us -> 864 us (1.050)
  waiting for transfers between devices: 312 us -> 356 us
  starting transfers between devices: 94.8 us -> 120 us
  local copies, waits for them, and re-layouts: 223 us -> 206 us
  other arithmetic: 155 us -> 143 us
    ppermute x0 -> x4, waiting for transfers between devices: none -> 169 us  [per_device(): lax.ppermute(totals, 'seq', [(dev, dev ^ hop) for dev in range(16)])]
    psum x1 -> x0, waiting for transfers between devices: 104 us -> none  [per_device(): totals = lax.psum(packed, 'seq')]
    ppermute x0 -> x4, starting transfers between devices: none -> 25.1 us  [per_device(): lax.ppermute(totals, 'seq', [(dev, dev ^ hop) for dev in range(16)])]
    reduce_scatter x1, waiting for transfers between devices: 93.7 us -> 72.5 us  [per_device(): shares = lax.psum_scatter(totals, 'dp', scatter_dimension=0, tiled=True)]
    mul x16, other arithmetic: 17.6 us -> 4.02 us  [pull_retreat(): adjoint = jnp.exp(a_trans * step_blk[position][None, :]) * gathered]
    mul x16, local copies, waits for them, and re-layouts: 9.97 us -> 0.13 us  [pull_retreat(): gathered = c_blk[position][:, None] * grad_blk[position][None, :] + adjoint]
  transfers between devices with their start and end apart: 32 -> 35, of which waited for: 32 -> 35; matrix products, arithmetic and copies ran while one was open for 0% -> 0% of each run, Pallas kernels for 0% -> 0%
where the time goes in v1:
time: 864 us; the launch traced here: 853 us
  waiting for transfers between devices  356 us (41%)
  local copies, waits for them, and re-layouts  206 us (24%)
  other arithmetic  143 us (17%)
  starting transfers between devices  120 us (14%)
  between operations  15.8 us (2%)
    ppermute x4, waiting for transfers between devices, per_device(): lax.ppermute(totals, 'seq', [(dev, dev ^ hop) for dev in range(16)])  169 us
    ppermute x30, waiting for transfers between devices, passed_along(): return lax.ppermute(block, axis, route)  114 us
    ppermute x30, starting transfers between devices, passed_along(): return lax.ppermute(block, axis, route)  94.7 us
    reduce_scatter x1, waiting for transfers between devices, per_device(): shares = lax.psum_scatter(totals, 'dp', scatter_dimension=0, tiled=True)  72.5 us
    slice x48, local copies, waits for them, and re-layouts, run_block(): val_blk[position]  69.5 us
    dynamic_slice x64, local copies, waits for them, and re-layouts, forward_record(): h_last, (checks, outputs) = lax.scan(advance, h_start, blocks)  44.5 us
    reduce_sum x80, other arithmetic, run_block(): outputs.append(jnp.sum(c_blk[position][:, None] * h_now, axis=0))  36.7 us
    reduce_sum x32, other arithmetic, run_block(): decay = jnp.exp(a_trans * step_blk[position][None, :])  33.3 us
  transfers between devices with their start and end apart: 35, of which 35 were waited for; matrix products, arithmetic and copies ran while one was open for 0% of the time, Pallas kernels for 0%

profile of v1, /device:TPU:1, one launch (start us, length us, event | category | flops | bytes accessed | tf_op | source)
XLA Modules:
  0.0 852.6 jit_solution(17661322087214478475)
XLA Ops:
  14.2 38.7 %while.126 = (s32[]{:T(128)}, f32[16,2048]{1,0:T(8,128)S(1)}, f32[16,8,2048]{2,1,0:T(8,128)}, f32[16,2048]{1,0:T(8,128)S(1)}, f32[16,8,16]{2,1,0:T(8,128)}, /*in...) while((s32[]{:T(128)}, f32[16,2048]{1,0:T(8,128)S(1)}, ...), condition=%wide.region_2.3_spmd.clone, body=%wide.region_1.2_spmd.clone.sunk | while | flops 1097738 | bytes 985871 | solution.py:37
  54.0 95.3 %while.123 = (s32[]{:T(128)}, f32[1,16,2048]{2,1,0:T(8,128)S(1)}, f32[1,16,2048]{2,1,0:T(8,128)S(1)}, f32[1,16,2048]{2,1,0:T(8,128)S(1)}, s32[]{:T(128)}) while((s32[]{:T(128)}, f32[1,16,2048]{2,1,0:T(8,128)S(1)}, f32[1,16,2048]{2,1,0:T(8,128)S(1)}, f32[1,16,2048]{2,1,0:T(8,128)S(1)}, s32[]{:T(128)}) %tuple.427), condition=%wide.region_4.5_spmd, body=%wide.region_3.4_spmd.sunk | while | flops 65538 | bytes 1048677 | solution.py:139
  150.4 73.6 %while.124 = (s32[]{:T(128)}, f32[16,2048]{1,0:T(8,128)S(1)}, f32[16,16,2048]{2,1,0:T(8,128)}, f32[16,8,2048]{2,1,0:T(8,128)}, f32[16,8,2048]{2,1,0:T(8,128)}, /...) while((s32[]{:T(128)}, f32[16,2048]{1,0:T(8,128)S(1)}, ...), condition=%wide.region_14.15_spmd, body=%wide.region_5.0_spmd.sunk | while | flops 2359305 | bytes 2333341 | solution.py:37
  227.5 43.2 %while.127 = (s32[]{:T(128)}, f32[16,2048]{1,0:T(8,128)S(1)}, f32[16,8,2048]{2,1,0:T(8,128)}, f32[16,2048]{1,0:T(8,128)S(1)}, f32[16,8,16]{2,1,0:T(8,128)}, /*in...) while((s32[]{:T(128)}, f32[16,2048]{1,0:T(8,128)S(1)}, ...), condition=%wide.region_16.17_spmd.clone, body=%wide.region_15.16_spmd.clone.sunk | while | flops 1081355 | bytes 789283 | solution.py:51
  270.7 114.7 %while.125 = (s32[]{:T(128)}, f32[1,16,2048]{2,1,0:T(8,128)S(1)}, f32[1,16,2048]{2,1,0:T(8,128)S(1)}, f32[1,16,2048]{2,1,0:T(8,128)S(1)}, s32[]{:T(128)}) while((s32[]{:T(128)}, f32[1,16,2048]{2,1,0:T(8,128)S(1)}, f32[1,16,2048]{2,1,0:T(8,128)S(1)}, f32[1,16,2048]{2,1,0:T(8,128)S(1)}, s32[]{:T(128)}) %tuple.426), condition=%wide.region_18.19_spmd, body=%wide.region_17.18_spmd.sunk | while | flops 65538 | bytes 1048677 | solution.py:140
  272.7 5.7 collective-permute-done.1
  287.8 6.3 collective-permute-done.1
  303.4 6.3 collective-permute-done.1
  319.0 6.3 collective-permute-done.1
  327.2 5.6 collective-permute-done.1
  334.8 5.6 collective-permute-done.1
  342.3 5.6 collective-permute-done.1
  349.8 5.6 collective-permute-done.1
  357.3 5.6 collective-permute-done.1
  364.9 5.6 collective-permute-done.1
  372.4 5.6 collective-permute-done.1
  379.9 5.6 collective-permute-done.1
  387.7 174.9 %while.128 = (s32[]{:T(128)}, f32[16,2048]{1,0:T(8,128)S(1)}, f32[16,2048]{1,0:T(8,128)S(1)}, f32[16,8,2048]{2,1,0:T(8,128)}, bf16[16,8,16]{2,1,0:T(8,128)(2,1)S...) while((s32[]{:T(128)}, f32[16,2048]{1,0:T(8,128)S(1)}, ...), condition=%wide.region_52.53_spmd.clone, body=%wide.region_19.52_spmd.clone.sunk | while | flops 8701451 | bytes 6086559 | solution.py:66
  571.1 7.4 collective-permute-start.3
  578.5 33.2 %collective-permute-done.3 = f32[2048,180]{0,1:T(8,128)S(1)} collective-permute-done((f32[2048,180]{0,1:T(8,128)S(1)}, f32[2048,180]{0,1:T(8,128)S(1)}, u32[]{:S(2)}, u32[]{:S(2)}) %collective-permute-start.3) | collective-permute-done | bytes 1474592 | tf_op jit(solution)/shard_map/ppermute | solution.py:194
  611.9 14.4 %collective-permute-start.4 = (f32[2048,180]{0,1:T(8,128)S(1)}, f32[2048,180]{0,1:T(8,128)S(1)}, u32[]{:S(2)}, u32[]{:S(2)}) collective-permute-start(f32[2048,180]{0,1:T(8,128)S(1)} %add.420), channel_id=1, source_target_pairs={{0,4},{1,5},{2,6},{3,7},{4,0},{5,1},{6,2},{7,3},{8,12},{9,13},{10,... | collective-permute-start | bytes 4423688 | tf_op jit(solution)/shard_map/ppermute | solution.py:194
  626.3 65.0 %collective-permute-done.4 = f32[2048,180]{0,1:T(8,128)S(1)} collective-permute-done((f32[2048,180]{0,1:T(8,128)S(1)}, f32[2048,180]{0,1:T(8,128)S(1)}, u32[]{:S(2)}, u32[]{:S(2)}) %collective-permute-start.4) | collective-permute-done | bytes 1474592 | tf_op jit(solution)/shard_map/ppermute | solution.py:194
  694.8 68.0 %collective-permute-done.5 = f32[2048,180]{0,1:T(8,128)S(1)} collective-permute-done((f32[2048,180]{0,1:T(8,128)S(1)}, f32[2048,180]{0,1:T(8,128)S(1)}, u32[]{:S(2)}, u32[]{:S(2)}) %collective-permute-start.5) | collective-permute-done | bytes 1474592 | tf_op jit(solution)/shard_map/ppermute | solution.py:194
  766.6 72.5 %reduce-scatter.2.cloned.1.call-done = f32[128,180]{0,1:T(8,128)} async-done(((f32[2048,180]{0,1:T(8,128)}), f32[128,180]{0,1:T(8,128)}) %reduce-scatter.2.cloned.1.call-update) | async-done | bytes 92176 | tf_op jit(solution)/shard_map/reduce_scatter | solution.py:195
  (1218 shorter events, 501.2 us)
Async XLA Ops:
  7.2 831.9 %reduce-scatter.2.cloned.1.call-start = ((), (), s32[]{:S(2)}) async-start(), calls=%async_computation.1 | async-start | bytes 1601536 | tf_op jit(solution)/shard_map/reduce_scatter | solution.py:195
  54.0 6.9 collective-permute-start
  60.9 6.3 collective-permute-start
  73.5 6.3 collective-permute-start
  92.5 6.3 collective-permute-start
  105.1 6.3 collective-permute-start
  270.8 7.6 collective-permute-start.1
  278.4 7.4 collective-permute-start.1
  285.8 8.2 collective-permute-start.1
  294.1 7.4 collective-permute-start.1
  301.5 8.2 collective-permute-start.1
  309.7 7.4 collective-permute-start.1
  317.1 8.2 collective-permute-start.1
  325.3 7.5 collective-permute-start.1
  332.8 7.5 collective-permute-start.1
  340.4 7.5 collective-permute-start.1
  347.9 7.5 collective-permute-start.1
  355.4 7.5 collective-permute-start.1
  362.9 7.5 collective-permute-start.1
  370.5 7.5 collective-permute-start.1
  378.0 7.5 collective-permute-start.1
  571.1 40.6 %collective-permute-start.3 = (f32[2048,180]{0,1:T(8,128)S(1)}, f32[2048,180]{0,1:T(8,128)S(1)}, u32[]{:S(2)}, u32[]{:S(2)}) collective-permute-start(f32[2048,180]{0,1:T(8,128)S(1)} %add.419), channel_id=1, source_target_pairs={{0,2},{1,3},{2,0},{3,1},{4,6},{5,7},{6,4},{7,5},{8,10},{9,11},{10,... | collective-permute-start | bytes 4423688 | tf_op jit(solution)/shard_map/ppermute | solution.py:194
  611.9 79.4 %collective-permute-start.4 = (f32[2048,180]{0,1:T(8,128)S(1)}, f32[2048,180]{0,1:T(8,128)S(1)}, u32[]{:S(2)}, u32[]{:S(2)}) collective-permute-start(f32[2048,180]{0,1:T(8,128)S(1)} %add.420), channel_id=1, source_target_pairs={{0,4},{1,5},{2,6},{3,7},{4,0},{5,1},{6,2},{7,3},{8,12},{9,13},{10,... | collective-permute-start | bytes 4423688 | tf_op jit(solution)/shard_map/ppermute | solution.py:194
  691.6 71.2 %collective-permute-start.5 = (f32[2048,180]{0,1:T(8,128)S(1)}, f32[2048,180]{0,1:T(8,128)S(1)}, u32[]{:S(2)}, u32[]{:S(2)}) collective-permute-start(f32[2048,180]{0,1:T(8,128)S(1)} %add.421), channel_id=1, source_target_pairs={{0,8},{1,9},{2,10},{3,11},{4,12},{5,13},{6,14},{7,15},{8,0},{9,1},... | collective-permute-start | bytes 4423688 | tf_op jit(solution)/shard_map/ppermute | solution.py:194
  (29 other events, 1161.3 us)
Sparse Core Ops, SparseCore 0:
  764.3 74.7 reduce-scatter.1
